TPU v7x, 128 devices: a whole 4x4x4 slice. The times are simulated.
128 devices in a mesh: section: 2 (over core), blk: 16 (over y, x), mp: 4 (over z).
Axes of the slice: x: 4, y: 4, z: 4, core: 2. Of those that a mesh axis runs over, the one named last changes fastest.
Arguments:
- patches: bfloat16 [256, 5120], P('section'), may hold values from -6 to 6
- merge_gain: float32 [1280], replicated, may hold values from 0.25 to 1.75
- merge_first: bfloat16 [5120, 5120], P(None, ('blk', 'mp')), may hold values from -0.078125 to 0.078125
- merge_second: bfloat16 [5120, 4096], P(('blk', 'mp')), may hold values from -0.078125 to 0.078125
- text_embeds: bfloat16 [4, 1024, 4096], P(None, 'blk', 'mp'), may hold values from -7 to 14
- positions: int32 [256], replicated, may hold values from 0 to 4095, as said below
- segments: int32 [4096], replicated, may hold values from 0 to 2, never falling along the last dimension, each value on 1 to 2048 neighbouring positions
- norm_gain: float32 [2, 4096], P('section'), may hold values from 0.25 to 1.75
- query_weight: bfloat16 [2, 4096, 4096], P('section', 'blk', 'mp'), may hold values from -1 to 1
- keyval_weight: bfloat16 [2, 4096, 4, 2, 128], P('section', 'blk', 'mp'), may hold values from -1 to 1
- out_weight: bfloat16 [2, 4096, 4096], P('section', 'mp', 'blk'), may hold values from -0.09375 to 0.09375
Outputs:
- hidden: bfloat16 [2, 4, 1024, 4096], P('section', None, 'blk', 'mp')
Inputs may be any that keep to these rules, and one draw needn't show every extreme that they name: `positions`: distinct and increasing.
All inputs are finite; a program needn't handle non-finite values.
Results may differ from a plain program's by a relative error of at most 0.015.
Values may be sent and summed in bfloat16 or wider, within the bound.
No kernel may reach another device: no remote copies, remote signals or barrier semaphores. Data moves between devices by JAX's collectives and lax.ppermute only.
A program may use at most 128 MiB of HBM per device.

v0:
```python
import jax
import jax.numpy as jnp
from jax import lax
from jax.sharding import PartitionSpec as P

epsilon = 1e-06
rope_base = 1000000.0


def shifted(value, axis, by):
    size = lax.axis_size(axis)
    pairs = [(i, i + by) for i in range(size) if 0 <= i + by < size]
    return lax.ppermute(value, axis, pairs)


def rope_tables(where_at, head_size):
    steps_half = jnp.arange(head_size // 2).astype(jnp.float32)
    inverse = jnp.exp(-jnp.log(rope_base) * 2.0 * steps_half / head_size)
    angles = where_at.astype(jnp.float32)[:, None] * inverse[None, :]
    return (jnp.cos(angles), jnp.sin(angles))


def rotate(values, cosine, sine):
    half = values.shape[-1] // 2
    first = values[..., :half]
    second = values[..., half:]
    cosine = cosine[:, None, :]
    sine = sine[:, None, :]
    return jnp.concatenate(
        [first * cosine - second * sine, second * cosine + first * sine], axis=-1
    )


def local(
    patches,
    merge_gain,
    merge_first,
    merge_second,
    text_embeds,
    positions,
    segments,
    norm_gain,
    query_weight,
    keyval_weight,
    out_weight,
):
    count = patches.shape[0]
    width = merge_gain.shape[0]
    blocks = text_embeds.shape[0]
    rows_here = text_embeds.shape[1]
    slice_width = text_embeds.shape[2]
    seq_len = segments.shape[0]
    block_len = seq_len // blocks
    section_index = lax.axis_index("section")
    cycle_index = lax.axis_index("blk")
    model_index = lax.axis_index("mp")
    pieces = patches.astype(jnp.float32).reshape(count, -1, width)
    centered = pieces - jnp.mean(pieces, axis=-1, keepdims=True)
    variance = jnp.mean(centered * centered, axis=-1, keepdims=True)
    normed = (
        (centered * lax.rsqrt(variance + epsilon) * merge_gain)
        .reshape(count, -1)
        .astype(jnp.bfloat16)
    )
    inner = jax.nn.gelu(
        jnp.dot(normed, merge_first, preferred_element_type=jnp.float32), approximate=False
    ).astype(jnp.bfloat16)
    partial_merge = jnp.dot(inner, merge_second, preferred_element_type=jnp.float32)
    merged_full = lax.psum(partial_merge, ("blk", "mp")).astype(jnp.bfloat16)
    merged_mine = lax.dynamic_slice_in_dim(merged_full, model_index * slice_width, slice_width, 1)
    visual_all = lax.all_gather(merged_mine, "section", axis=0, tiled=True)
    query_full, keyval_full, out_full = (
        lax.all_gather(query_weight, "blk", axis=1, tiled=True),
        lax.all_gather(keyval_weight, "blk", axis=1, tiled=True),
        lax.all_gather(out_weight, "blk", axis=2, tiled=True),
    )
    query_full = query_full[0]
    kv_heads = keyval_full.shape[2]
    head_size = keyval_full.shape[4]
    keyval_full = keyval_full[0].reshape(keyval_full.shape[1], -1)
    out_full = out_full[0]
    gain_here = norm_gain[0]
    group = query_full.shape[1] // (kv_heads * head_size)
    scale = 1.0 / head_size**0.5
    key_where = jnp.arange(seq_len)
    ticks = blocks + lax.axis_size("section") - 1
    zero_index = jnp.zeros((), jnp.int32)
    held = jnp.zeros((rows_here, slice_width), jnp.bfloat16)
    cache_keys = jnp.zeros((seq_len, kv_heads, head_size), jnp.bfloat16)
    cache_values = jnp.zeros((seq_len, kv_heads, head_size), jnp.bfloat16)
    outputs = jnp.zeros((blocks, rows_here, slice_width), jnp.bfloat16)
    for tick_now in range(ticks):
        bound = min(tick_now + 1, blocks) * block_len
        block_now = tick_now - section_index
        active = (block_now >= 0) & (block_now < blocks)
        block_safe = jnp.clip(block_now, 0, blocks - 1)
        row_where = block_safe * block_len + cycle_index * rows_here + jnp.arange(rows_here)
        is_visual = positions[None, :] == row_where[:, None]
        picked = jnp.dot(
            is_visual.astype(jnp.bfloat16), visual_all, preferred_element_type=jnp.float32
        ).astype(jnp.bfloat16)
        text_rows = lax.dynamic_index_in_dim(text_embeds, block_safe, 0, keepdims=False)
        embedded = jnp.where(jnp.any(is_visual, axis=1)[:, None], picked, text_rows)
        incoming = jnp.where(section_index == 0, embedded, held)
        features = lax.all_gather(incoming, "mp", axis=1, tiled=True)
        feat_f = features.astype(jnp.float32)
        normx = (
            feat_f
            * lax.rsqrt(jnp.mean(feat_f * feat_f, axis=-1, keepdims=True) + epsilon)
            * gain_here
        ).astype(jnp.bfloat16)
        cosine, sine = rope_tables(row_where, head_size)
        query = jnp.dot(normx, query_full, preferred_element_type=jnp.float32).reshape(
            rows_here, -1, head_size
        )
        query = (
            rotate(query, cosine, sine)
            .astype(jnp.bfloat16)
            .reshape(rows_here, kv_heads, group, head_size)
        )
        keyval = jnp.dot(normx, keyval_full, preferred_element_type=jnp.float32).reshape(
            rows_here, kv_heads, 2, head_size
        )
        new_keys = rotate(keyval[:, :, 0, :], cosine, sine).astype(jnp.bfloat16)
        new_values = keyval[:, :, 1, :].astype(jnp.bfloat16)
        block_keys, block_values = (
            lax.all_gather(new_keys, "blk", axis=0, tiled=True),
            lax.all_gather(new_values, "blk", axis=0, tiled=True),
        )
        start = block_safe * block_len
        cache_keys = jnp.where(
            active,
            lax.dynamic_update_slice(cache_keys, block_keys, (start, zero_index, zero_index)),
            cache_keys,
        )
        cache_values = jnp.where(
            active,
            lax.dynamic_update_slice(cache_values, block_values, (start, zero_index, zero_index)),
            cache_values,
        )
        keys_seen = cache_keys[:bound]
        values_seen = cache_values[:bound]
        scores = (
            jnp.einsum("qkgd,skd->kgqs", query, keys_seen, preferred_element_type=jnp.float32)
            * scale
        )
        row_segments = jnp.take(segments, row_where)
        allowed = (key_where[None, :bound] <= row_where[:, None]) & (
            segments[None, :bound] == row_segments[:, None]
        )
        scores = jnp.where(allowed[None, None], scores, -jnp.inf)
        top = jnp.max(scores, axis=-1, keepdims=True)
        expo = jnp.exp(scores - top)
        probs = (expo / jnp.sum(expo, axis=-1, keepdims=True)).astype(jnp.bfloat16)
        attended = jnp.einsum(
            "kgqs,skd->qkgd", probs, values_seen, preferred_element_type=jnp.float32
        )
        attended = attended.reshape(rows_here, -1).astype(jnp.bfloat16)
        term = jnp.dot(attended, out_full, preferred_element_type=jnp.float32)
        summed = lax.psum_scatter(
            term.astype(jnp.bfloat16), "mp", scatter_dimension=1, tiled=True
        ).astype(jnp.float32)
        result = (incoming.astype(jnp.float32) + summed).astype(jnp.bfloat16)
        outputs = jnp.where(
            active,
            lax.dynamic_update_slice(outputs, result[None], (block_safe, zero_index, zero_index)),
            outputs,
        )
        held = shifted(result, "section", 1)
    return outputs[None]


def solution(mesh):
    return jax.shard_map(
        local,
        mesh=mesh,
        in_specs=(
            P("section", None),
            P(),
            P(None, ("blk", "mp")),
            P(("blk", "mp"), None),
            P(None, "blk", "mp"),
            P(),
            P(),
            P("section", None),
            P("section", "blk", "mp"),
            P("section", "blk", "mp", None, None),
            P("section", "mp", "blk"),
        ),
        out_specs=P("section", None, "blk", "mp"),
        check_vma=False,
    )
```

profile of v0, /device:TPU:0, one launch (start us, length us, event | category | flops | bytes accessed | tf_op | source)
XLA Modules:
  0.0 948.9 jit_solution(6913599249277682439)
XLA Ops:
  23.5 383.3 %all-reduce.1 = bf16[128,4096]{1,0:T(8,128)(2,1)S(1)} all-reduce(f32[128,4096]{1,0:T(8,128)} %fusion.210), channel_id=1, replica_groups=mesh['section'=2,'blk'=16,'mp'=4] {'blk','mp'}, use_global_device_ids=true, to_apply=%region_3.4 | all-reduce | flops 524288 | bytes 3145728 | tf_op jit(solution)/shard_map/psum | solution.py:69
  411.0 13.4 %all_gather.58 = bf16[64,4096]{1,0:T(8,128)(2,1)S(1)} all-gather(bf16[64,1024]{1,0:T(8,128)(2,1)S(1)} %fusion.63), channel_id=1, replica_groups=mesh['section'=2,'blk'=16,'mp'=4] {'mp'}, dimensions={1}, use_global_device_ids=true | all-gather | bytes 655360 | tf_op jit(solution)/shard_map/all_gather | solution.py:105
  432.0 20.7 %all_gather.61 = bf16[1024,1,128]{2,0,1:T(8,128)(2,1)S(1)} all-gather(bf16[64,1,128]{2,0,1:T(8,128)(2,1)S(1)} %pad_maximum_fusion), channel_id=1, replica_groups=mesh['section'=2,'blk'=16,'mp'=4] {'blk'}, dimensions={0}, use_global_device_ids=true | all-gather | bytes 278528 | tf_op jit(solution)/shard_map/all_gather | solution.py:127
  452.7 24.1 %all-gather = bf16[1024,1,1,128]{3,0,2,1:T(8,128)(2,1)S(1)} all-gather(bf16[64,1,1,128]{3,0,2,1:T(8,128)(2,1)S(1)} %slice.285), channel_id=2, replica_groups=mesh['section'=2,'blk'=16,'mp'=4] {'blk'}, dimensions={0}, use_global_device_ids=true | all-gather | bytes 278528 | tf_op jit(solution)/shard_map/all_gather | solution.py:128
  480.5 11.8 %copy.31 = bf16[1024,4096]{1,0:T(8,128)(2,1)} copy(bf16[1024,4096]{0,1:T(8,128)(2,1)} %bitcast.333) | data formatting | bytes 16777216 | tf_op jit(solution)/shard_map/dot_general | solution.py:113
  511.2 15.4 %reduce-scatter.6.cloned.1.call-done = bf16[64,1024]{1,0:T(8,128)(2,1)} async-done(((bf16[64,4096]{1,0:T(8,128)(2,1)}), bf16[64,1024]{1,0:T(8,128)(2,1)}) %reduce-scatter.6.cloned.1.call-update) | async-done | bytes 131088 | tf_op jit(solution)/shard_map/reduce_scatter | solution.py:160
  531.9 13.5 %all_gather.64 = bf16[64,4096]{1,0:T(8,128)(2,1)S(1)} all-gather(bf16[64,1024]{1,0:T(8,128)(2,1)S(1)} %fusion.65), channel_id=1, replica_groups=mesh['section'=2,'blk'=16,'mp'=4] {'mp'}, dimensions={1}, use_global_device_ids=true | all-gather | bytes 655360 | tf_op jit(solution)/shard_map/all_gather | solution.py:105
  552.6 23.8 %all-gather.1 = bf16[1024,1,1,128]{3,0,2,1:T(8,128)(2,1)S(1)} all-gather(bf16[64,1,1,128]{3,0,2,1:T(8,128)(2,1)S(1)} %slice.284), channel_id=3, replica_groups=mesh['section'=2,'blk'=16,'mp'=4] {'blk'}, dimensions={0}, use_global_device_ids=true | all-gather | bytes 278528 | tf_op jit(solution)/shard_map/all_gather | solution.py:128
  576.7 23.3 %all_gather.66 = bf16[1024,1,128]{2,0,1:T(8,128)(2,1)S(1)} all-gather(bf16[64,1,128]{2,0,1:T(8,128)(2,1)S(1)} %pad_maximum_fusion.1), channel_id=1, replica_groups=mesh['section'=2,'blk'=16,'mp'=4] {'blk'}, dimensions={0}, use_global_device_ids=true | all-gather | bytes 278528 | tf_op jit(solution)/shard_map/all_gather | solution.py:127
  616.2 14.5 %reduce-scatter.8.cloned.1.call-done = bf16[64,1024]{1,0:T(8,128)(2,1)} async-done(((bf16[64,4096]{1,0:T(8,128)(2,1)}), bf16[64,1024]{1,0:T(8,128)(2,1)}) %reduce-scatter.8.cloned.1.call-update) | async-done | bytes 131088 | tf_op jit(solution)/shard_map/reduce_scatter | solution.py:160
  633.9 13.5 %all_gather.67 = bf16[64,4096]{1,0:T(8,128)(2,1)S(1)} all-gather(bf16[64,1024]{1,0:T(8,128)(2,1)S(1)} %broadcast_select_fusion.2), channel_id=1, replica_groups=mesh['section'=2,'blk'=16,'mp'=4] {'mp'}, dimensions={1}, use_global_device_ids=true | all-gather | bytes 655360 | tf_op jit(solution)/shard_map/all_gather | solution.py:105
  648.5 6.1 fusion.131
  654.6 23.8 %all-gather.2 = bf16[1024,1,1,128]{3,0,2,1:T(8,128)(2,1)S(1)} all-gather(bf16[64,1,1,128]{3,0,2,1:T(8,128)(2,1)S(1)} %slice.283), channel_id=4, replica_groups=mesh['section'=2,'blk'=16,'mp'=4] {'blk'}, dimensions={0}, use_global_device_ids=true | all-gather | bytes 278528 | tf_op jit(solution)/shard_map/all_gather | solution.py:128
  678.7 23.4 %all_gather.69 = bf16[1024,1,128]{2,0,1:T(8,128)(2,1)S(1)} all-gather(bf16[64,1,128]{2,0,1:T(8,128)(2,1)S(1)} %pad_maximum_fusion.2), channel_id=1, replica_groups=mesh['section'=2,'blk'=16,'mp'=4] {'blk'}, dimensions={0}, use_global_device_ids=true | all-gather | bytes 278528 | tf_op jit(solution)/shard_map/all_gather | solution.py:127
  715.8 17.7 %reduce-scatter.10.cloned.1.call-done = bf16[64,1024]{1,0:T(8,128)(2,1)} async-done(((bf16[64,4096]{1,0:T(8,128)(2,1)}), bf16[64,1024]{1,0:T(8,128)(2,1)}) %reduce-scatter.10.cloned.1.call-update) | async-done | bytes 131088 | tf_op jit(solution)/shard_map/reduce_scatter | solution.py:160
  737.7 13.4 %all_gather.70 = bf16[64,4096]{1,0:T(8,128)(2,1)S(1)} all-gather(bf16[64,1024]{1,0:T(8,128)(2,1)S(1)} %broadcast_select_fusion.1), channel_id=1, replica_groups=mesh['section'=2,'blk'=16,'mp'=4] {'mp'}, dimensions={1}, use_global_device_ids=true | all-gather | bytes 655360 | tf_op jit(solution)/shard_map/all_gather | solution.py:105
  752.1 6.1 fusion.134
  758.2 23.8 %all-gather.3 = bf16[1024,1,1,128]{3,0,2,1:T(8,128)(2,1)S(1)} all-gather(bf16[64,1,1,128]{3,0,2,1:T(8,128)(2,1)S(1)} %slice.282), channel_id=5, replica_groups=mesh['section'=2,'blk'=16,'mp'=4] {'blk'}, dimensions={0}, use_global_device_ids=true | all-gather | bytes 278528 | tf_op jit(solution)/shard_map/all_gather | solution.py:128
  782.3 23.2 %all_gather.72 = bf16[1024,1,128]{2,0,1:T(8,128)(2,1)S(1)} all-gather(bf16[64,1,128]{2,0,1:T(8,128)(2,1)S(1)} %pad_maximum_fusion.3), channel_id=1, replica_groups=mesh['section'=2,'blk'=16,'mp'=4] {'blk'}, dimensions={0}, use_global_device_ids=true | all-gather | bytes 278528 | tf_op jit(solution)/shard_map/all_gather | solution.py:127
  818.7 18.8 %reduce-scatter.12.cloned.1.call-done = bf16[64,1024]{1,0:T(8,128)(2,1)} async-done(((bf16[64,4096]{1,0:T(8,128)(2,1)}), bf16[64,1024]{1,0:T(8,128)(2,1)}) %reduce-scatter.12.cloned.1.call-update) | async-done | bytes 131088 | tf_op jit(solution)/shard_map/reduce_scatter | solution.py:160
  844.1 12.8 %all_gather.73 = bf16[64,4096]{1,0:T(8,128)(2,1)S(1)} all-gather(bf16[64,1024]{1,0:T(8,128)(2,1)S(1)} %broadcast_select_fusion), channel_id=1, replica_groups=mesh['section'=2,'blk'=16,'mp'=4] {'mp'}, dimensions={1}, use_global_device_ids=true | all-gather | bytes 655360 | tf_op jit(solution)/shard_map/all_gather | solution.py:105
  864.0 23.8 %all-gather.4 = bf16[1024,1,1,128]{3,0,2,1:T(8,128)(2,1)S(1)} all-gather(bf16[64,1,1,128]{3,0,2,1:T(8,128)(2,1)S(1)} %slice.281), channel_id=6, replica_groups=mesh['section'=2,'blk'=16,'mp'=4] {'blk'}, dimensions={0}, use_global_device_ids=true | all-gather | bytes 278528 | tf_op jit(solution)/shard_map/all_gather | solution.py:128
  888.0 23.3 %all_gather.75 = bf16[1024,1,128]{2,0,1:T(8,128)(2,1)S(1)} all-gather(bf16[64,1,128]{2,0,1:T(8,128)(2,1)S(1)} %pad_maximum_fusion.4), channel_id=1, replica_groups=mesh['section'=2,'blk'=16,'mp'=4] {'blk'}, dimensions={0}, use_global_device_ids=true | all-gather | bytes 278528 | tf_op jit(solution)/shard_map/all_gather | solution.py:127
  922.1 18.1 %reduce-scatter.14.cloned.1.call-done = bf16[64,1024]{1,0:T(8,128)(2,1)} async-done(((bf16[64,4096]{1,0:T(8,128)(2,1)}), bf16[64,1024]{1,0:T(8,128)(2,1)}) %reduce-scatter.14.cloned.1.call-update) | async-done | bytes 131088 | tf_op jit(solution)/shard_map/reduce_scatter | solution.py:160
  (316 shorter events, 142.5 us)
Async XLA Ops:
  6.5 419.6 %all-gather.9.cloned.1.call-start = ((), (), s32[]{:S(2)}) async-start(), calls=%async_computation.5 | async-start | bytes 2228224 | tf_op jit(solution)/shard_map/all_gather | solution.py:74
  7.3 473.2 %all-gather.11.cloned.1.call-start = ((), (), s32[]{:S(2)}) async-start(), calls=%async_computation.6 | async-start | bytes 8912896 | tf_op jit(solution)/shard_map/all_gather | solution.py:73
  8.0 494.1 %all-gather.13.cloned.1.call-start = ((), (), s32[]{:S(2)}) async-start(), calls=%async_computation.7 | async-start | bytes 8912896 | tf_op jit(solution)/shard_map/all_gather | solution.py:75
  8.7 517.9 %reduce-scatter.6.cloned.1.call-start = ((), (), s32[]{:S(2)}) async-start(), calls=%async_computation.8 | async-start | bytes 655360 | tf_op jit(solution)/shard_map/reduce_scatter | solution.py:160
  21.4 385.4 %copy-start.25 = (s32[256]{0:T(256)S(1)}, s32[256]{0:T(256)}, u32[]{:S(2)}) copy-start(s32[256]{0:T(256)} %param.18) | copy-start | bytes 3076
  21.4 403.2 %slice-start.8 = ((s32[4096]{0:T(1024)}), s32[1024]{0:T(1024)S(1)}, s32[]{:S(2)}) async-start(s32[4096]{0:T(1024)} %param.19), calls=%async_computation.21 | async-start | bytes 8192 | tf_op jit(solution)/shard_map/slice | solution.py:149
  21.4 404.6 %copy-start.46 = (f32[64]{0:T(128)}, f32[64]{0:T(128)S(1)}, u32[]{:S(2)}) copy-start(f32[64]{0:T(128)S(1)} %get-tuple-element.74) | copy-start | bytes 772
  22.2 554.2 %copy-start.26 = (f32[64]{0:T(128)}, f32[64]{0:T(128)S(1)}, u32[]{:S(2)}) copy-start(f32[64]{0:T(128)S(1)} %multiply_exponential_fusion) | copy-start | bytes 772
  22.2 384.6 %copy-start.44 = (s32[64]{0:T(128)}, s32[64]{0:T(128)S(1)}, u32[]{:S(2)}) copy-start(s32[64]{0:T(128)S(1)} %iota_add_fusion.5) | copy-start | bytes 772
  22.3 384.5 %copy-start.29 = (s32[64]{0:T(128)}, s32[64]{0:T(128)S(1)}, u32[]{:S(2)}) copy-start(s32[64]{0:T(128)S(1)} %get-tuple-element.77) | copy-start | bytes 772
  22.3 403.8 %copy-start.40 = (f32[64]{0:T(128)}, f32[64]{0:T(128)S(1)}, u32[]{:S(2)}) copy-start(f32[64]{0:T(128)S(1)} %get-tuple-element.80) | copy-start | bytes 772
  22.3 403.8 %copy-start.42 = (f32[64]{0:T(128)}, f32[64]{0:T(128)S(1)}, u32[]{:S(2)}) copy-start(f32[64]{0:T(128)S(1)} %get-tuple-element.79) | copy-start | bytes 772
  22.3 384.5 %copy-start.32 = (s32[64]{0:T(128)}, s32[64]{0:T(128)S(1)}, u32[]{:S(2)}) copy-start(s32[64]{0:T(128)S(1)} %get-tuple-element.75) | copy-start | bytes 772
  22.3 384.5 %copy-start.34 = (s32[64]{0:T(128)}, s32[64]{0:T(128)S(1)}, u32[]{:S(2)}) copy-start(s32[64]{0:T(128)S(1)} %get-tuple-element.76) | copy-start | bytes 772
  22.3 403.7 %copy-start.36 = (f32[64]{0:T(128)}, f32[64]{0:T(128)S(1)}, u32[]{:S(2)}) copy-start(f32[64]{0:T(128)S(1)} %get-tuple-element.82) | copy-start | bytes 772
  22.4 403.7 %copy-start.38 = (f32[64]{0:T(128)}, f32[64]{0:T(128)S(1)}, u32[]{:S(2)}) copy-start(f32[64]{0:T(128)S(1)} %get-tuple-element.81) | copy-start | bytes 772
  508.0 122.6 %reduce-scatter.8.cloned.1.call-start = ((), (), s32[]{:S(2)}) async-start(), calls=%async_computation.9 | async-start | bytes 655360 | tf_op jit(solution)/shard_map/reduce_scatter | solution.py:160
  527.7 2.4 collective-permute-start
  611.8 121.7 %reduce-scatter.10.cloned.1.call-start = ((), (), s32[]{:S(2)}) async-start(), calls=%async_computation.10 | async-start | bytes 655360 | tf_op jit(solution)/shard_map/reduce_scatter | solution.py:160
  631.6 2.3 collective-permute-start.1
  714.5 122.9 %reduce-scatter.12.cloned.1.call-start = ((), (), s32[]{:S(2)}) async-start(), calls=%async_computation.11 | async-start | bytes 655360 | tf_op jit(solution)/shard_map/reduce_scatter | solution.py:160
  734.5 2.5 collective-permute-start.2
  818.6 121.5 %reduce-scatter.14.cloned.1.call-start = ((), (), s32[]{:S(2)}) async-start(), calls=%async_computation.12 | async-start | bytes 655360 | tf_op jit(solution)/shard_map/reduce_scatter | solution.py:160
  838.5 4.9 collective-permute-start.3
  (58 other events, 1124.9 us)
Sparse Core Ops, SparseCore 0:
  9.5 47.7 all-gather.8
  59.5 74.0 all-gather.10
  135.7 81.8 all-gather.12
  508.1 18.4 reduce-scatter.5
  611.9 18.7 reduce-scatter.7
  714.6 18.8 reduce-scatter.9
  818.8 18.6 reduce-scatter.11
  921.4 18.7 reduce-scatter.13
where the time goes:
time: 957 us; the launch traced here: 949 us
  blocking collectives  685 us (72%)
  waiting for transfers between devices  87 us (9%)
  matrix products  81.5 us (9%)
  other arithmetic  37.5 us (4%)
  local copies, waits for them, and re-layouts  37.3 us (4%)
  between operations  15.1 us (2%)
    psum x1, blocking collectives, local(): merged_full = lax.psum(partial_merge, ('blk', 'mp')).astype(jnp.bfloat16)  383 us
    all_gather x5, blocking collectives, local(): lax.all_gather(new_values, 'blk', axis=0, tiled=True)  119 us
    all_gather x5, blocking collectives, local(): lax.all_gather(new_keys, 'blk', axis=0, tiled=True)  114 us
    reduce_scatter x5, waiting for transfers between devices, local(): lax.psum_scatter(term.astype(jnp.bfloat16), 'mp', scatter_dimension=1, ti...  84.4 us
    all_gather x5, blocking collectives, local(): features = lax.all_gather(incoming, 'mp', axis=1, tiled=True)  66.5 us
    dot_general x5, matrix products, local(): jnp.dot(normx, query_full, preferred_element_type=jnp.float32)  30.4 us
  transfers between devices with their start and end apart: 12, of which 6 were waited for; matrix products, arithmetic and copies ran while one was open for 7% of the time, Pallas kernels for 0%

commit v1 on v0

--- a/solution.py
+++ b/solution.py
@@ -5,6 +5,15 @@
 
 epsilon = 1e-06
 rope_base = 1000000.0
+
+
+def post_columns(row_data, mesh_ax):
+    gallery = []
+    for _ in range(lax.axis_size(mesh_ax)):
+        gallery.append(row_data)
+    x_next = jnp.stack(gallery)
+    y1 = lax.all_to_all(x_next, concat_axis=0, split_axis=0, axis_name=mesh_ax)
+    return jnp.concatenate(y1, axis=0)
 
 
 def shifted(value, axis, by):
@@ -125,7 +134,7 @@
         new_values = keyval[:, :, 1, :].astype(jnp.bfloat16)
         block_keys, block_values = (
             lax.all_gather(new_keys, "blk", axis=0, tiled=True),
-            lax.all_gather(new_values, "blk", axis=0, tiled=True),
+            post_columns(new_values, "blk"),
         )
         start = block_safe * block_len
         cache_keys = jnp.where(

time: 957 us -> 919 us (0.960)
  blocking collectives: 685 us -> 574 us
  starting transfers between devices: 5.47 us -> 37.1 us
  matrix products: 81.5 us -> 101 us
  local copies, waits for them, and re-layouts: 37.3 us -> 53.2 us
    all_gather x5 -> x0, blocking collectives: 119 us -> none  [local(): lax.all_gather(new_values, 'blk', axis=0, tiled=True)]
    all_to_all x0 -> x5, starting transfers between devices: none -> 31.6 us  [post_columns(): y1 = lax.all_to_all(x_next, concat_axis=0, split_axis=0, axis_name=mesh_ax)]
    unnamed x139 -> x127, local copies, waits for them, and re-layouts: 9.62 us -> 21.4 us
    dot_general x5, matrix products: 15.2 us -> 25.5 us  [local(): term = jnp.dot(attended, out_full, preferred_element_type=jnp.float32)]
  transfers between devices with their start and end apart: 12 -> 17, of which waited for: 6 -> 6; matrix products, arithmetic and copies ran while one was open for 7% -> 10% of each run, Pallas kernels for 0% -> 0%
where the time goes in v1:
time: 919 us; the launch traced here: 911 us
  blocking collectives  574 us (62%)
  matrix products  101 us (11%)
  waiting for transfers between devices  90.7 us (10%)
  local copies, waits for them, and re-layouts  53.2 us (6%)
  other arithmetic  40.6 us (4%)
  starting transfers between devices  37.1 us (4%)
  between operations  15.1 us (2%)
    psum x1, blocking collectives, local(): merged_full = lax.psum(partial_merge, ('blk', 'mp')).astype(jnp.bfloat16)  383 us
    all_gather x5, blocking collectives, local(): lax.all_gather(new_keys, 'blk', axis=0, tiled=True)  121 us
    reduce_scatter x5, waiting for transfers between devices, local(): lax.psum_scatter(term.astype(jnp.bfloat16), 'mp', scatter_dimension=1, ti...  88 us
    all_gather x5, blocking collectives, local(): features = lax.all_gather(incoming, 'mp', axis=1, tiled=True)  66.5 us
    all_to_all x5, starting transfers between devices, post_columns(): y1 = lax.all_to_all(x_next, concat_axis=0, split_axis=0, axis_name=mesh_ax)  31.6 us
    dot_general x5, matrix products, local(): jnp.dot(normx, query_full, preferred_element_type=jnp.float32)  31.1 us
    dot_general x5, matrix products, local(): term = jnp.dot(attended, out_full, preferred_element_type=jnp.float32)  25.5 us
    unnamed x127, local copies, waits for them, and re-layouts  21.4 us
  transfers between devices with their start and end apart: 17, of which 6 were waited for; matrix products, arithmetic and copies ran while one was open for 10% of the time, Pallas kernels for 0%

profile of v1, /device:TPU:0, one launch (start us, length us, event | category | flops | bytes accessed | tf_op | source)
XLA Modules:
  0.0 910.8 jit_solution(10592025570657899442)
XLA Ops:
  23.5 383.5 %all-reduce.1 = bf16[128,4096]{1,0:T(8,128)(2,1)S(1)} all-reduce(f32[128,4096]{1,0:T(8,128)} %fusion.207), channel_id=1, replica_groups=mesh['section'=2,'blk'=16,'mp'=4] {'blk','mp'}, use_global_device_ids=true, to_apply=%region_3.4 | all-reduce | flops 524288 | bytes 3145728 | tf_op jit(solution)/shard_map/psum | solution.py:78
  411.2 13.4 %all_gather.43 = bf16[64,4096]{1,0:T(8,128)(2,1)S(1)} all-gather(bf16[64,1024]{1,0:T(8,128)(2,1)S(1)} %fusion.63), channel_id=1, replica_groups=mesh['section'=2,'blk'=16,'mp'=4] {'mp'}, dimensions={1}, use_global_device_ids=true | all-gather | bytes 655360 | tf_op jit(solution)/shard_map/all_gather | solution.py:114
  437.2 24.2 %all_gather.45 = bf16[1024,1,128]{2,0,1:T(8,128)(2,1)S(1)} all-gather(bf16[64,1,128]{2,0,1:T(8,128)(2,1)S(1)} %pad_maximum_fusion), channel_id=1, replica_groups=mesh['section'=2,'blk'=16,'mp'=4] {'blk'}, dimensions={0}, use_global_device_ids=true | all-gather | bytes 278528 | tf_op jit(solution)/shard_map/all_gather | solution.py:136
  466.1 11.3 %copy.31 = bf16[1024,4096]{1,0:T(8,128)(2,1)} copy(bf16[1024,4096]{0,1:T(8,128)(2,1)} %bitcast.324) | data formatting | bytes 16777216 | tf_op jit(solution)/shard_map/dot_general | solution.py:122
  477.4 6.1 fusion.125
  496.3 16.4 %reduce-scatter.6.cloned.1.call-done = bf16[64,1024]{1,0:T(8,128)(2,1)} async-done(((bf16[64,4096]{1,0:T(8,128)(2,1)}), bf16[64,1024]{1,0:T(8,128)(2,1)}) %reduce-scatter.6.cloned.1.call-update) | async-done | bytes 131088 | tf_op jit(solution)/shard_map/reduce_scatter | solution.py:169
  518.0 13.5 %all_gather.48 = bf16[64,4096]{1,0:T(8,128)(2,1)S(1)} all-gather(bf16[64,1024]{1,0:T(8,128)(2,1)S(1)} %fusion.65), channel_id=1, replica_groups=mesh['section'=2,'blk'=16,'mp'=4] {'mp'}, dimensions={1}, use_global_device_ids=true | all-gather | bytes 655360 | tf_op jit(solution)/shard_map/all_gather | solution.py:114
  539.4 6.9 all-to-all-start.1
  546.6 24.3 %all_gather.49 = bf16[1024,1,128]{2,0,1:T(8,128)(2,1)S(1)} all-gather(bf16[64,1,128]{2,0,1:T(8,128)(2,1)S(1)} %pad_maximum_fusion.1), channel_id=1, replica_groups=mesh['section'=2,'blk'=16,'mp'=4] {'blk'}, dimensions={0}, use_global_device_ids=true | all-gather | bytes 278528 | tf_op jit(solution)/shard_map/all_gather | solution.py:136
  590.6 15.2 %reduce-scatter.8.cloned.1.call-done = bf16[64,1024]{1,0:T(8,128)(2,1)} async-done(((bf16[64,4096]{1,0:T(8,128)(2,1)}), bf16[64,1024]{1,0:T(8,128)(2,1)}) %reduce-scatter.8.cloned.1.call-update) | async-done | bytes 131088 | tf_op jit(solution)/shard_map/reduce_scatter | solution.py:169
  609.0 13.5 %all_gather.50 = bf16[64,4096]{1,0:T(8,128)(2,1)S(1)} all-gather(bf16[64,1024]{1,0:T(8,128)(2,1)S(1)} %broadcast_select_fusion.3), channel_id=1, replica_groups=mesh['section'=2,'blk'=16,'mp'=4] {'mp'}, dimensions={1}, use_global_device_ids=true | all-gather | bytes 655360 | tf_op jit(solution)/shard_map/all_gather | solution.py:114
  630.5 6.8 all-to-all-start.2
  637.7 24.5 %all_gather.51 = bf16[1024,1,128]{2,0,1:T(8,128)(2,1)S(1)} all-gather(bf16[64,1,128]{2,0,1:T(8,128)(2,1)S(1)} %pad_maximum_fusion.2), channel_id=1, replica_groups=mesh['section'=2,'blk'=16,'mp'=4] {'blk'}, dimensions={0}, use_global_device_ids=true | all-gather | bytes 278528 | tf_op jit(solution)/shard_map/all_gather | solution.py:136
  684.0 18.3 %reduce-scatter.10.cloned.1.call-done = bf16[64,1024]{1,0:T(8,128)(2,1)} async-done(((bf16[64,4096]{1,0:T(8,128)(2,1)}), bf16[64,1024]{1,0:T(8,128)(2,1)}) %reduce-scatter.10.cloned.1.call-update) | async-done | bytes 131088 | tf_op jit(solution)/shard_map/reduce_scatter | solution.py:169
  706.4 13.4 %all_gather.52 = bf16[64,4096]{1,0:T(8,128)(2,1)S(1)} all-gather(bf16[64,1024]{1,0:T(8,128)(2,1)S(1)} %broadcast_select_fusion.2), channel_id=1, replica_groups=mesh['section'=2,'blk'=16,'mp'=4] {'mp'}, dimensions={1}, use_global_device_ids=true | all-gather | bytes 655360 | tf_op jit(solution)/shard_map/all_gather | solution.py:114
  720.8 6.8 fusion.134
  728.4 6.9 all-to-all-start.3
  735.6 24.2 %all_gather.53 = bf16[1024,1,128]{2,0,1:T(8,128)(2,1)S(1)} all-gather(bf16[64,1,128]{2,0,1:T(8,128)(2,1)S(1)} %pad_maximum_fusion.3), channel_id=1, replica_groups=mesh['section'=2,'blk'=16,'mp'=4] {'blk'}, dimensions={0}, use_global_device_ids=true | all-gather | bytes 278528 | tf_op jit(solution)/shard_map/all_gather | solution.py:136
  783.0 19.5 %reduce-scatter.12.cloned.1.call-done = bf16[64,1024]{1,0:T(8,128)(2,1)} async-done(((bf16[64,4096]{1,0:T(8,128)(2,1)}), bf16[64,1024]{1,0:T(8,128)(2,1)}) %reduce-scatter.12.cloned.1.call-update) | async-done | bytes 131088 | tf_op jit(solution)/shard_map/reduce_scatter | solution.py:169
  811.2 12.8 %all_gather.54 = bf16[64,4096]{1,0:T(8,128)(2,1)S(1)} all-gather(bf16[64,1024]{1,0:T(8,128)(2,1)S(1)} %broadcast_select_fusion.1), channel_id=1, replica_groups=mesh['section'=2,'blk'=16,'mp'=4] {'mp'}, dimensions={1}, use_global_device_ids=true | all-gather | bytes 655360 | tf_op jit(solution)/shard_map/all_gather | solution.py:114
  825.0 6.1 fusion.137
  831.9 6.8 all-to-all-start.4
  839.1 24.3 %all_gather.55 = bf16[1024,1,128]{2,0,1:T(8,128)(2,1)S(1)} all-gather(bf16[64,1,128]{2,0,1:T(8,128)(2,1)S(1)} %pad_maximum_fusion.4), channel_id=1, replica_groups=mesh['section'=2,'blk'=16,'mp'=4] {'blk'}, dimensions={0}, use_global_device_ids=true | all-gather | bytes 278528 | tf_op jit(solution)/shard_map/all_gather | solution.py:136
  883.4 18.7 %reduce-scatter.14.cloned.1.call-done = bf16[64,1024]{1,0:T(8,128)(2,1)} async-done(((bf16[64,4096]{1,0:T(8,128)(2,1)}), bf16[64,1024]{1,0:T(8,128)(2,1)}) %reduce-scatter.14.cloned.1.call-update) | async-done | bytes 131088 | tf_op jit(solution)/shard_map/reduce_scatter | solution.py:169
  (312 shorter events, 178.4 us)
Async XLA Ops:
  6.5 419.8 %all-gather.4.cloned.1.call-start = ((), (), s32[]{:S(2)}) async-start(), calls=%async_computation.10 | async-start | bytes 2228224 | tf_op jit(solution)/shard_map/all_gather | solution.py:83
  7.3 458.8 %all-gather.6.cloned.1.call-start = ((), (), s32[]{:S(2)}) async-start(), calls=%async_computation.11 | async-start | bytes 8912896 | tf_op jit(solution)/shard_map/all_gather | solution.py:82
  8.0 479.3 %all-gather.8.cloned.1.call-start = ((), (), s32[]{:S(2)}) async-start(), calls=%async_computation.12 | async-start | bytes 8912896 | tf_op jit(solution)/shard_map/all_gather | solution.py:84
  21.4 403.5 %slice-start.2 = ((s32[4096]{0:T(1024)}), s32[1024]{0:T(1024)S(1)}, s32[]{:S(2)}) async-start(s32[4096]{0:T(1024)} %param.19), calls=%async_computation.20 | async-start | bytes 8192 | tf_op jit(solution)/shard_map/slice | solution.py:158
  21.4 404.9 %copy-start.46 = (f32[64]{0:T(128)}, f32[64]{0:T(128)S(1)}, u32[]{:S(2)}) copy-start(f32[64]{0:T(128)S(1)} %get-tuple-element.74) | copy-start | bytes 772
  22.2 524.1 %copy-start.26 = (f32[64]{0:T(128)}, f32[64]{0:T(128)S(1)}, u32[]{:S(2)}) copy-start(f32[64]{0:T(128)S(1)} %multiply_exponential_fusion) | copy-start | bytes 772
  22.2 404.1 %copy-start.40 = (f32[64]{0:T(128)}, f32[64]{0:T(128)S(1)}, u32[]{:S(2)}) copy-start(f32[64]{0:T(128)S(1)} %get-tuple-element.80) | copy-start | bytes 772
  22.3 404.1 %copy-start.42 = (f32[64]{0:T(128)}, f32[64]{0:T(128)S(1)}, u32[]{:S(2)}) copy-start(f32[64]{0:T(128)S(1)} %get-tuple-element.79) | copy-start | bytes 772
  22.3 404.0 %copy-start.36 = (f32[64]{0:T(128)}, f32[64]{0:T(128)S(1)}, u32[]{:S(2)}) copy-start(f32[64]{0:T(128)S(1)} %get-tuple-element.82) | copy-start | bytes 772
  22.3 404.0 %copy-start.38 = (f32[64]{0:T(128)}, f32[64]{0:T(128)S(1)}, u32[]{:S(2)}) copy-start(f32[64]{0:T(128)S(1)} %get-tuple-element.81) | copy-start | bytes 772
  432.7 30.6 %all-to-all-start = ((bf16[16,64,1,128]{3,1,2,0:T(8,128)(2,1)}), bf16[16,64,1,128]{3,1,2,0:T(8,128)(2,1)}, u32[]{:S(2)}, u32[]{:S(2)}) async-start(bf16[16,64,1,128]{3,1,2,0:T(8,128)(2,1)} %stack.10), calls=%async_computation | async-start | bytes 524288 | tf_op jit(solution)/shard_map/all_to_all | solution.py:15
  436.9 75.8 %reduce-scatter.6.cloned.1.call-start = ((), (), s32[]{:S(2)}) async-start(), calls=%async_computation.13 | async-start | bytes 655360 | tf_op jit(solution)/shard_map/reduce_scatter | solution.py:169
  513.7 2.5 collective-permute-start
  539.4 38.8 %all-to-all-start.1 = ((bf16[16,64,1,128]{3,1,2,0:T(8,128)(2,1)}), bf16[16,64,1,128]{3,1,2,0:T(8,128)(2,1)}, u32[]{:S(2)}, u32[]{:S(2)}) async-start(bf16[16,64,1,128]{3,1,2,0:T(8,128)(2,1)} %stack.11), calls=%async_computation.2 | async-start | bytes 524288 | tf_op jit(solution)/shard_map/all_to_all | solution.py:15
  546.3 59.5 %reduce-scatter.8.cloned.1.call-start = ((), (), s32[]{:S(2)}) async-start(), calls=%async_computation.14 | async-start | bytes 655360 | tf_op jit(solution)/shard_map/reduce_scatter | solution.py:169
  606.7 2.3 collective-permute-start.1
  630.5 40.4 %all-to-all-start.2 = ((bf16[16,64,1,128]{3,1,2,0:T(8,128)(2,1)}), bf16[16,64,1,128]{3,1,2,0:T(8,128)(2,1)}, u32[]{:S(2)}, u32[]{:S(2)}) async-start(bf16[16,64,1,128]{3,1,2,0:T(8,128)(2,1)} %stack.12), calls=%async_computation.4 | async-start | bytes 524288 | tf_op jit(solution)/shard_map/all_to_all | solution.py:15
  637.3 64.9 %reduce-scatter.10.cloned.1.call-start = ((), (), s32[]{:S(2)}) async-start(), calls=%async_computation.15 | async-start | bytes 655360 | tf_op jit(solution)/shard_map/reduce_scatter | solution.py:169
  703.3 2.5 collective-permute-start.2
  728.4 41.9 %all-to-all-start.3 = ((bf16[16,64,1,128]{3,1,2,0:T(8,128)(2,1)}), bf16[16,64,1,128]{3,1,2,0:T(8,128)(2,1)}, u32[]{:S(2)}, u32[]{:S(2)}) async-start(bf16[16,64,1,128]{3,1,2,0:T(8,128)(2,1)} %stack.13), calls=%async_computation.6 | async-start | bytes 524288 | tf_op jit(solution)/shard_map/all_to_all | solution.py:15
  735.2 67.2 %reduce-scatter.12.cloned.1.call-start = ((), (), s32[]{:S(2)}) async-start(), calls=%async_computation.16 | async-start | bytes 655360 | tf_op jit(solution)/shard_map/reduce_scatter | solution.py:169
  803.5 7.0 collective-permute-start.3
  831.9 38.9 %all-to-all-start.4 = ((bf16[16,64,1,128]{3,1,2,0:T(8,128)(2,1)}), bf16[16,64,1,128]{3,1,2,0:T(8,128)(2,1)S(1)}, u32[]{:S(2)}, u32[]{:S(2)}) async-start(bf16[16,64,1,128]{3,1,2,0:T(8,128)(2,1)} %stack.14), calls=%async_computation.8 | async-start | bytes 524288 | tf_op jit(solution)/shard_map/all_to_all | solution.py:15
  838.8 63.3 %reduce-scatter.14.cloned.1.call-start = ((), (), s32[]{:S(2)}) async-start(), calls=%async_computation.17 | async-start | bytes 655360 | tf_op jit(solution)/shard_map/reduce_scatter | solution.py:169
  (57 other events, 2614.5 us)
Sparse Core Ops, SparseCore 0:
  9.5 47.7 all-gather.3
  59.5 74.0 all-gather.5
  135.7 81.6 all-gather.7
  493.3 19.3 reduce-scatter.5
  586.4 19.3 reduce-scatter.7
  682.8 19.3 reduce-scatter.9
  783.1 19.3 reduce-scatter.11
  882.7 19.3 reduce-scatter.13
